TPU v7x, 256 devices: a whole 4x4x8 slice. The times are simulated.
256 devices in a mesh: gx: 64 (over z, x, core), gy: 4 (over y).
Axes of the slice: x: 4, y: 4, z: 8, core: 2. Of those that a mesh axis runs over, the one named last changes fastest.
Arguments:
- pressure: float32 [512, 512, 128], P('gx', 'gy'), may hold values from -6 to 8
- vel_y: float32 [512, 512, 128], P('gx', 'gy'), may hold values from -6 to 6
- vel_z: float32 [512, 512, 128], P('gx', 'gy'), may hold values from -6 to 6
- material: int32 [512, 512, 128], P('gx', 'gy'), may hold values from 0 to 7
- absorb_table: float32 [8], replicated, may hold values from 0.02 to 4
Outputs:
- pressure_next: float32 [512, 512, 128], P('gx', 'gy')
- vel_y_next: float32 [512, 512, 128], P('gx', 'gy')
- vel_z_next: float32 [512, 512, 128], P('gx', 'gy')
All inputs are finite; a program needn't handle non-finite values.
Results may differ from a plain program's by a relative error of at most 0.0004.
Values sent between devices are 32-bit elements; how exact they have to be, the bound alone decides.
A program may use at most 128 MiB of HBM per device.

v0:
```python
import jax
import jax.numpy as jnp
from jax import lax
from jax.sharding import PartitionSpec as P

MATS = 8


def passed_along(value, axis, steps):
    count = lax.axis_size(axis)
    first, last = (max(0, -steps), min(count, count - steps))
    return lax.ppermute(value, axis, [(source, source + steps) for source in range(first, last)])


def join_segments(left, right):
    denom = 1.0 - left[5] * right[1]
    inner_const = (left[3] + left[5] * right[0]) / denom
    inner_left = left[4] / denom
    inner_right = left[5] * right[2] / denom
    outer_const = right[0] + right[1] * inner_const
    outer_left = right[1] * inner_left
    outer_right = right[2] + right[1] * inner_right
    return (
        left[0] + left[2] * outer_const,
        left[1] + left[2] * outer_left,
        left[2] * outer_right,
        right[3] + right[4] * inner_const,
        right[4] * inner_left,
        right[5] + right[4] * inner_right,
    )


def sweep_lines(excess, stacked):

    def forward(carry, items):
        carried, value_prev = carry
        excess_row, value_row = items
        inverse = 1.0 / (1.0 + excess_row + carried)
        value = (value_row + value_prev) * inverse[None]
        carried_next = (excess_row + carried) * inverse
        return ((carried_next, value), (inverse, value))

    start = (jnp.ones(excess.shape[1:], jnp.float32), jnp.zeros(stacked.shape[1:], jnp.float32))
    _, (inverses, values) = lax.scan(forward, start, (excess, stacked))

    def backward(following, items):
        inverse, value = items
        current = value + inverse[None] * following
        return (current, current)

    _, solved = lax.scan(
        backward, jnp.zeros(stacked.shape[1:], jnp.float32), (inverses, values), reverse=True
    )
    return solved


def body(pressure, vel_y, vel_z, material, absorb_table):
    absorb = jnp.zeros(pressure.shape, jnp.float32)
    for entry in range(MATS):
        absorb = absorb + jnp.where(material == entry, absorb_table[entry], 0.0)
    damping = 1.0 / (1.0 + absorb)
    above = passed_along(pressure[:, :1, :], "gy", -1)
    upper_y = jnp.concatenate([pressure[:, 1:, :], above], axis=1)
    upper_z = jnp.concatenate([pressure[:, :, 1:], jnp.zeros_like(pressure[:, :, :1])], axis=2)
    vel_y_next = damping * (vel_y - 0.5 * (upper_y - pressure))
    vel_z_next = damping * (vel_z - 0.5 * (upper_z - pressure))
    below = passed_along(vel_y_next[:, -1:, :], "gy", 1)
    lower_y = jnp.concatenate([below, vel_y_next[:, :-1, :]], axis=1)
    lower_z = jnp.concatenate([jnp.zeros_like(pressure[:, :, :1]), vel_z_next[:, :, :-1]], axis=2)
    source = pressure - 0.5 * (vel_y_next - lower_y + vel_z_next - lower_z)
    line_cells = pressure.shape[0] * lax.axis_size("gx")
    coupling = 1.0 * (line_cells * line_cells // 4)
    excess = (1.0 + absorb) / coupling
    scaled = source / coupling
    rows = lax.broadcasted_iota(jnp.int32, pressure.shape, 0)
    first_unit = jnp.where(rows == 0, -1.0, 0.0)
    last_unit = jnp.where(rows == pressure.shape[0] - 1, -1.0, 0.0)
    stacked = jnp.stack([scaled, first_unit, last_unit], axis=1)
    solved = sweep_lines(excess, stacked)
    local_part = solved[:, 0]
    left_spike = solved[:, 1]
    right_spike = solved[:, 2]
    own = (
        local_part[0],
        -left_spike[0],
        -right_spike[0],
        local_part[-1],
        -left_spike[-1],
        -right_spike[-1],
    )
    nothing = jnp.zeros(local_part.shape[1:], jnp.float32)
    single = jnp.ones(local_part.shape[1:], jnp.float32)
    identity = (nothing, nothing, single, nothing, single, nothing)
    table = (
        lax.all_gather(own[0][None], "gx", axis=0, tiled=True),
        lax.all_gather(own[1][None], "gx", axis=0, tiled=True),
        lax.all_gather(own[2][None], "gx", axis=0, tiled=True),
        lax.all_gather(own[3][None], "gx", axis=0, tiled=True),
        lax.all_gather(own[4][None], "gx", axis=0, tiled=True),
        lax.all_gather(own[5][None], "gx", axis=0, tiled=True),
    )
    position = lax.axis_index("gx")
    indices = jnp.arange(lax.axis_size("gx"), dtype=jnp.int32)

    def take_lower(carry, items):
        index, pieces = items
        merged = join_segments(carry, pieces)
        keep = index < position
        return (tuple((jnp.where(keep, fresh, older) for fresh, older in zip(merged, carry))), None)

    def take_higher(carry, items):
        index, pieces = items
        merged = join_segments(pieces, carry)
        keep = index > position
        return (tuple((jnp.where(keep, fresh, older) for fresh, older in zip(merged, carry))), None)

    prefix, _ = lax.scan(take_lower, identity, (indices, table))
    suffix, _ = lax.scan(take_higher, identity, (indices, table), reverse=True)
    top_rhs = own[0] + own[1] * prefix[3] + own[2] * suffix[0]
    bottom_rhs = own[3] + own[4] * prefix[3] + own[5] * suffix[0]
    top_top = 1.0 - own[1] * prefix[5]
    top_bottom = -own[2] * suffix[1]
    bottom_top = -own[4] * prefix[5]
    bottom_bottom = 1.0 - own[5] * suffix[1]
    determinant = top_top * bottom_bottom - top_bottom * bottom_top
    top_value = (top_rhs * bottom_bottom - top_bottom * bottom_rhs) / determinant
    bottom_value = (top_top * bottom_rhs - bottom_top * top_rhs) / determinant
    before_value = prefix[3] + prefix[5] * top_value
    after_value = suffix[0] + suffix[1] * bottom_value
    pressure_next = local_part - left_spike * before_value[None] - right_spike * after_value[None]
    return (pressure_next, vel_y_next, vel_z_next)


def solution(mesh):
    return jax.shard_map(
        body,
        mesh=mesh,
        in_specs=(
            P("gx", "gy", None),
            P("gx", "gy", None),
            P("gx", "gy", None),
            P("gx", "gy", None),
            P(),
        ),
        out_specs=(P("gx", "gy", None), P("gx", "gy", None), P("gx", "gy", None)),
        check_vma=False,
    )
```

profile of v0, /device:TPU:1, one launch (start us, length us, event | category | flops | bytes accessed | tf_op | source)
XLA Modules:
  0.0 848.9 jit_solution(11246831425350953470)
XLA Ops:
  8.1 1.3 collective-permute-start
  9.4 1.6 fusion.49
  11.0 1.1 slice.93
  12.1 1.2 slice.97
  13.4 6.4 fusion.32
  19.8 4.6 collective-permute-start.1
  25.8 1.4 broadcast.68.clone
  27.2 20.3 %while.64 = (s32[]{:T(128)}, f32[128,128]{1,0:T(8,128)S(1)}, f32[3,128,128]{2,1,0:T(8,128)S(1)}, f32[8,128,128]{2,1,0:T(8,128)S(1)}, f32[8,3,128,128]{3,2,1,0:T(...) while((s32[]{:T(128)}, f32[128,128]{1,0:T(8,128)S(1)}, ...), condition=%wide.region_1.2_spmd.clone, body=%wide.region_0.1_spmd.clone.sunk | while | flops 262147 | bytes 1376881 | solution.py:44
  48.5 15.2 %while.65 = (s32[]{:T(128)}, f32[3,128,128]{2,1,0:T(8,128)S(1)}, f32[8,3,128,128]{3,2,1,0:T(8,128)S(1)}, f32[8,3,128,128]{3,2,1,0:T(8,128)}, f32[8,128,128]{2,1,0:T(8,128)}, /*index=5*/s32[]{:T(128)}, s32[]{:T(128)}, s32[]{:T(128)}) while((s32[]{:T(128)}, f32[3,128,128]{2,1,0:T(8,128)S(1)}, f32[8,3,128,128]{3,2,1,0:T(8,128)S(1)}, ...), condition=%wide.region_3.4_spmd.clone, body=%wide.region_2.3_spmd.clone.sunk | while | flops 147460 | bytes 983155 | solution.py:51
  67.7 81.3 %all-gather.13.cloned.1.call-done = f32[64,1,128,128]{3,2,1,0:T(8,128)} async-done(((f32[1,1,128,128]{3,2,1,0:T(8,128)}), f32[64,1,128,128]{3,2,1,0:T(8,128)}) %all-gather.13.cloned.1.call-update) | async-done | bytes 4194320 | tf_op jit(solution)/shard_map/all_gather | solution.py:98
  149.1 79.5 %all-gather.15.cloned.1.call-done = f32[64,1,128,128]{3,2,1,0:T(8,128)} async-done(((f32[1,1,128,128]{3,2,1,0:T(8,128)}), f32[64,1,128,128]{3,2,1,0:T(8,128)}) %all-gather.15.cloned.1.call-update) | async-done | bytes 4194320 | tf_op jit(solution)/shard_map/all_gather | solution.py:99
  228.6 79.0 %all-gather.17.cloned.1.call-done = f32[64,1,128,128]{3,2,1,0:T(8,128)} async-done(((f32[1,1,128,128]{3,2,1,0:T(8,128)}), f32[64,1,128,128]{3,2,1,0:T(8,128)}) %all-gather.17.cloned.1.call-update) | async-done | bytes 4194320 | tf_op jit(solution)/shard_map/all_gather | solution.py:95
  307.6 78.8 %all-gather.19.cloned.1.call-done = f32[64,1,128,128]{3,2,1,0:T(8,128)} async-done(((f32[1,1,128,128]{3,2,1,0:T(8,128)}), f32[64,1,128,128]{3,2,1,0:T(8,128)}) %all-gather.19.cloned.1.call-update) | async-done | bytes 4194320 | tf_op jit(solution)/shard_map/all_gather | solution.py:96
  386.4 78.8 %all-gather.21.cloned.1.call-done = f32[64,1,128,128]{3,2,1,0:T(8,128)} async-done(((f32[1,1,128,128]{3,2,1,0:T(8,128)}), f32[64,1,128,128]{3,2,1,0:T(8,128)}) %all-gather.21.cloned.1.call-update) | async-done | bytes 4194320 | tf_op jit(solution)/shard_map/all_gather | solution.py:100
  465.2 78.8 %all-gather.23.cloned.1.call-done = f32[64,1,128,128]{3,2,1,0:T(8,128)} async-done(((f32[1,1,128,128]{3,2,1,0:T(8,128)}), f32[64,1,128,128]{3,2,1,0:T(8,128)}) %all-gather.23.cloned.1.call-update) | async-done | bytes 4194320 | tf_op jit(solution)/shard_map/all_gather | solution.py:97
  544.0 148.7 %while.67 = (s32[]{:T(128)}, f32[128,128]{1,0:T(8,128)S(1)}, f32[128,128]{1,0:T(8,128)S(1)}, s32[64]{0:T(128)S(1)}, s32[]{:T(128)}, /*index=5*/f32[64,128,128]{2...) while((s32[]{:T(128)}, f32[128,128]{1,0:T(8,128)S(1)}, ...), condition=%wide.region_7.8_spmd.clone, body=%wide.region_6.7_spmd.clone.sunk | while | flops 278533 | bytes 655541 | solution.py:118
  545.3 1.1 fusion.56
  547.6 1.1 fusion.56
  549.9 1.1 fusion.56
  552.3 1.1 fusion.56
  554.6 1.1 fusion.56
  556.9 1.1 fusion.56
  559.2 1.1 fusion.56
  561.5 1.1 fusion.56
  563.9 1.1 fusion.56
  566.2 1.1 fusion.56
  568.5 1.1 fusion.56
  570.8 1.1 fusion.56
  573.2 1.1 fusion.56
  575.5 1.1 fusion.56
  577.8 1.1 fusion.56
  580.1 1.1 fusion.56
  582.5 1.1 fusion.56
  584.8 1.1 fusion.56
  587.1 1.1 fusion.56
  589.4 1.1 fusion.56
  591.7 1.1 fusion.56
  594.1 1.1 fusion.56
  596.4 1.1 fusion.56
  598.7 1.1 fusion.56
  601.0 1.1 fusion.56
  603.4 1.1 fusion.56
  605.7 1.1 fusion.56
  608.0 1.1 fusion.56
  610.3 1.1 fusion.56
  612.7 1.1 fusion.56
  615.0 1.1 fusion.56
  617.3 1.1 fusion.56
  619.6 1.1 fusion.56
  621.9 1.1 fusion.56
  624.3 1.1 fusion.56
  626.6 1.1 fusion.56
  628.9 1.1 fusion.56
  631.2 1.1 fusion.56
  633.6 1.1 fusion.56
  635.9 1.1 fusion.56
  638.2 1.1 fusion.56
  640.5 1.1 fusion.56
  642.9 1.1 fusion.56
  645.2 1.1 fusion.56
  647.5 1.1 fusion.56
  649.8 1.1 fusion.56
  652.1 1.1 fusion.56
  692.7 148.3 %while.66 = (s32[]{:T(128)}, f32[128,128]{1,0:T(8,128)S(1)}, f32[128,128]{1,0:T(8,128)S(1)}, s32[64]{0:T(128)S(1)}, s32[]{:T(128)}, /*index=5*/f32[64,128,128]{2...) while((s32[]{:T(128)}, f32[128,128]{1,0:T(8,128)S(1)}, ...), condition=%wide.region_5.6_spmd.clone, body=%wide.region_4.5_spmd.clone.sunk | while | flops 245764 | bytes 655521 | solution.py:117
  (299 shorter events, 204.0 us)
Async XLA Ops:
  7.2 6.2 copy-start
  7.2 6.2 copy-start.4
  7.2 6.2 copy-start.5
  7.2 141.9 %all-gather.13.cloned.1.call-start = ((), (), s32[]{:S(2)}) async-start(), calls=%async_computation | async-start | bytes 4259840 | tf_op jit(solution)/shard_map/all_gather | solution.py:98
  7.2 6.2 copy-start.6
  8.1 5.2 collective-permute-start
  19.8 5.7 copy-start.1
  19.8 5.7 copy-start.2
  19.8 5.4 collective-permute-start.1
  47.5 0.8 copy-start.3
  64.5 164.2 %all-gather.15.cloned.1.call-start = ((), (), s32[]{:S(2)}) async-start(), calls=%async_computation.1 | async-start | bytes 4259840 | tf_op jit(solution)/shard_map/all_gather | solution.py:99
  65.2 242.4 %all-gather.17.cloned.1.call-start = ((), (), s32[]{:S(2)}) async-start(), calls=%async_computation.2 | async-start | bytes 4259840 | tf_op jit(solution)/shard_map/all_gather | solution.py:95
  65.9 320.5 %all-gather.19.cloned.1.call-start = ((), (), s32[]{:S(2)}) async-start(), calls=%async_computation.3 | async-start | bytes 4259840 | tf_op jit(solution)/shard_map/all_gather | solution.py:96
  66.5 398.7 %all-gather.21.cloned.1.call-start = ((), (), s32[]{:S(2)}) async-start(), calls=%async_computation.4 | async-start | bytes 4259840 | tf_op jit(solution)/shard_map/all_gather | solution.py:100
  67.1 476.9 %all-gather.23.cloned.1.call-start = ((), (), s32[]{:S(2)}) async-start(), calls=%async_computation.5 | async-start | bytes 4259840 | tf_op jit(solution)/shard_map/all_gather | solution.py:97
Sparse Core Ops, SparseCore 0:
  64.6 84.4 all-gather.12
  152.4 76.1 all-gather.14
  231.4 76.1 all-gather.16
  310.2 76.1 all-gather.18
  389.0 76.1 all-gather.20
  467.8 76.1 all-gather.22
where the time goes:
time: 859 us; the launch traced here: 849 us
  waiting for transfers between devices  480 us (56%)
  other arithmetic  172 us (20%)
  local copies, waits for them, and re-layouts  89.3 us (10%)
  loops' own time  86.8 us (10%)
  between operations  14.4 us (2%)
    all_gather x1, waiting for transfers between devices, body(): lax.all_gather(own[3][None], 'gx', axis=0, tiled=True)  81.3 us
    all_gather x1, waiting for transfers between devices, body(): lax.all_gather(own[4][None], 'gx', axis=0, tiled=True)  79.5 us
    all_gather x1, waiting for transfers between devices, body(): lax.all_gather(own[0][None], 'gx', axis=0, tiled=True)  79 us
    all_gather x1, waiting for transfers between devices, body(): lax.all_gather(own[2][None], 'gx', axis=0, tiled=True)  78.8 us
    all_gather x1, waiting for transfers between devices, body(): lax.all_gather(own[1][None], 'gx', axis=0, tiled=True)  78.8 us
    all_gather x1, waiting for transfers between devices, body(): lax.all_gather(own[5][None], 'gx', axis=0, tiled=True)  78.8 us
    dynamic_slice x128, local copies, waits for them, and re-layouts, body(): prefix, _ = lax.scan(take_lower, identity, (indices, table))  75.1 us
    select_n x64, other arithmetic, take_higher(): jnp.where(keep, fresh, older)  67.8 us
  transfers between devices with their start and end apart: 8, of which 7 were waited for; matrix products, arithmetic and copies ran while one was open for 0% of the time, Pallas kernels for 0%

commit v1 on v0

--- a/solution.py
+++ b/solution.py
@@ -94,7 +94,9 @@
     table = (
         lax.all_gather(own[0][None], "gx", axis=0, tiled=True),
         lax.all_gather(own[1][None], "gx", axis=0, tiled=True),
-        lax.all_gather(own[2][None], "gx", axis=0, tiled=True),
+        jnp.concatenate(
+            lax.all_to_all(jnp.stack([own[2][None]] * lax.axis_size("gx")), "gx", 0, 0), axis=0
+        ),
         lax.all_gather(own[3][None], "gx", axis=0, tiled=True),
         lax.all_gather(own[4][None], "gx", axis=0, tiled=True),
         lax.all_gather(own[5][None], "gx", axis=0, tiled=True),

time: 859 us -> 801 us (0.932)
  waiting for transfers between devices: 480 us -> 406 us
  starting transfers between devices: 6.16 us -> 19.8 us
    all_to_all x0 -> x1, waiting for transfers between devices: none -> 106 us  [body(): lax.all_to_all(jnp.stack([own[2][None]] * lax.axis_size('gx')), 'gx', 0, 0)]
    all_gather x1, waiting for transfers between devices: 81.3 us -> 0.01 us  [body(): lax.all_gather(own[3][None], 'gx', axis=0, tiled=True)]
    all_gather x1 -> x0, waiting for transfers between devices: 78.8 us -> none  [body(): lax.all_gather(own[2][None], 'gx', axis=0, tiled=True)]
    all_gather x1, waiting for transfers between devices: 79.5 us -> 60.5 us  [body(): lax.all_gather(own[4][None], 'gx', axis=0, tiled=True)]
    all_to_all x0 -> x1, starting transfers between devices: none -> 13.6 us  [body(): lax.all_to_all(jnp.stack([own[2][None]] * lax.axis_size('gx')), 'gx', 0, 0)]
  transfers between devices with their start and end apart: 8 -> 8, of which waited for: 7 -> 6; matrix products, arithmetic and copies ran while one was open for 0% -> 1% of each run, Pallas kernels for 0% -> 0%
where the time goes in v1:
time: 801 us; the launch traced here: 791 us
  waiting for transfers between devices  406 us (51%)
  other arithmetic  172 us (21%)
  local copies, waits for them, and re-layouts  91.8 us (11%)
  loops' own time  86.8 us (11%)
  starting transfers between devices  19.8 us (2%)
  between operations  14.1 us (2%)
    all_to_all x1, waiting for transfers between devices, body(): lax.all_to_all(jnp.stack([own[2][None]] * lax.axis_size('gx')), 'gx', 0, 0)  106 us
    all_gather x1, waiting for transfers between devices, body(): lax.all_gather(own[0][None], 'gx', axis=0, tiled=True)  79 us
    all_gather x1, waiting for transfers between devices, body(): lax.all_gather(own[1][None], 'gx', axis=0, tiled=True)  78.8 us
    all_gather x1, waiting for transfers between devices, body(): lax.all_gather(own[5][None], 'gx', axis=0, tiled=True)  78.8 us
    dynamic_slice x128, local copies, waits for them, and re-layouts, body(): prefix, _ = lax.scan(take_lower, identity, (indices, table))  75.1 us
    select_n x64, other arithmetic, take_higher(): jnp.where(keep, fresh, older)  67.8 us
    select_n x64, other arithmetic, take_lower(): jnp.where(keep, fresh, older)  67.8 us
    all_gather x1, waiting for transfers between devices, body(): lax.all_gather(own[4][None], 'gx', axis=0, tiled=True)  60.5 us
  transfers between devices with their start and end apart: 8, of which 6 were waited for; matrix products, arithmetic and copies ran while one was open for 1% of the time, Pallas kernels for 0%

profile of v1, /device:TPU:1, one launch (start us, length us, event | category | flops | bytes accessed | tf_op | source)
XLA Modules:
  0.0 791.0 jit_solution(223411861730702953)
XLA Ops:
  8.1 1.3 collective-permute-start
  9.4 1.6 fusion.49
  11.0 1.1 slice.93
  12.1 1.2 slice.97
  13.4 6.3 fusion.32
  19.8 4.6 collective-permute-start.1
  25.8 1.4 broadcast.70.clone
  27.2 20.3 %while.64 = (s32[]{:T(128)}, f32[128,128]{1,0:T(8,128)S(1)}, f32[3,128,128]{2,1,0:T(8,128)S(1)}, f32[8,128,128]{2,1,0:T(8,128)S(1)}, f32[8,3,128,128]{3,2,1,0:T(...) while((s32[]{:T(128)}, f32[128,128]{1,0:T(8,128)S(1)}, ...), condition=%wide.region_1.2_spmd.clone, body=%wide.region_0.1_spmd.clone.sunk | while | flops 262147 | bytes 1376881 | solution.py:44
  48.5 15.2 %while.65 = (s32[]{:T(128)}, f32[3,128,128]{2,1,0:T(8,128)S(1)}, f32[8,3,128,128]{3,2,1,0:T(8,128)S(1)}, f32[8,3,128,128]{3,2,1,0:T(8,128)}, f32[8,128,128]{2,1,0:T(8,128)}, /*index=5*/s32[]{:T(128)}, s32[]{:T(128)}, s32[]{:T(128)}) while((s32[]{:T(128)}, f32[3,128,128]{2,1,0:T(8,128)S(1)}, f32[8,3,128,128]{3,2,1,0:T(8,128)S(1)}, ...), condition=%wide.region_3.4_spmd.clone, body=%wide.region_2.3_spmd.clone.sunk | while | flops 147460 | bytes 983155 | solution.py:51
  66.5 2.5 stack.16
  69.0 13.6 %all-to-all-start = ((f32[64,1,128,128]{3,2,1,0:T(8,128)}), f32[64,1,128,128]{3,2,1,0:T(8,128)}, u32[]{:S(2)}, u32[]{:S(2)}) async-start(f32[64,1,128,128]{3,2,1,0:T(8,128)} %stack.16), calls=%async_computation | async-start | bytes 8388608 | tf_op jit(solution)/shard_map/all_to_all | solution.py:98
  83.3 105.9 %all-to-all-done = f32[64,1,128,128]{3,2,1,0:T(8,128)} async-done(((f32[64,1,128,128]{3,2,1,0:T(8,128)}), f32[64,1,128,128]{3,2,1,0:T(8,128)}, u32[]{:S(2)}, u32[]{:S(2)}) %all-to-all-start) | async-done | bytes 4194336 | tf_op jit(solution)/shard_map/all_to_all | solution.py:98
  189.2 60.5 %all-gather.13.cloned.1.call-done = f32[64,1,128,128]{3,2,1,0:T(8,128)} async-done(((f32[1,1,128,128]{3,2,1,0:T(8,128)}), f32[64,1,128,128]{3,2,1,0:T(8,128)}) %all-gather.13.cloned.1.call-update) | async-done | bytes 4194320 | tf_op jit(solution)/shard_map/all_gather | solution.py:101
  249.7 79.0 %all-gather.15.cloned.1.call-done = f32[64,1,128,128]{3,2,1,0:T(8,128)} async-done(((f32[1,1,128,128]{3,2,1,0:T(8,128)}), f32[64,1,128,128]{3,2,1,0:T(8,128)}) %all-gather.15.cloned.1.call-update) | async-done | bytes 4194320 | tf_op jit(solution)/shard_map/all_gather | solution.py:95
  328.6 78.8 %all-gather.17.cloned.1.call-done = f32[64,1,128,128]{3,2,1,0:T(8,128)} async-done(((f32[1,1,128,128]{3,2,1,0:T(8,128)}), f32[64,1,128,128]{3,2,1,0:T(8,128)}) %all-gather.17.cloned.1.call-update) | async-done | bytes 4194320 | tf_op jit(solution)/shard_map/all_gather | solution.py:96
  407.5 78.8 %all-gather.19.cloned.1.call-done = f32[64,1,128,128]{3,2,1,0:T(8,128)} async-done(((f32[1,1,128,128]{3,2,1,0:T(8,128)}), f32[64,1,128,128]{3,2,1,0:T(8,128)}) %all-gather.19.cloned.1.call-update) | async-done | bytes 4194320 | tf_op jit(solution)/shard_map/all_gather | solution.py:102
  486.3 148.7 %while.67 = (s32[]{:T(128)}, f32[128,128]{1,0:T(8,128)S(1)}, f32[128,128]{1,0:T(8,128)S(1)}, s32[64]{0:T(128)S(1)}, s32[]{:T(128)}, /*index=5*/f32[64,128,128]{2...) while((s32[]{:T(128)}, f32[128,128]{1,0:T(8,128)S(1)}, ...), condition=%wide.region_7.8_spmd.clone, body=%wide.region_6.7_spmd.clone.sunk | while | flops 278533 | bytes 655541 | solution.py:120
  487.5 1.1 fusion.56
  489.8 1.1 fusion.56
  492.2 1.1 fusion.56
  494.5 1.1 fusion.56
  496.8 1.1 fusion.56
  499.1 1.1 fusion.56
  501.5 1.1 fusion.56
  503.8 1.1 fusion.56
  506.1 1.1 fusion.56
  508.4 1.1 fusion.56
  510.8 1.1 fusion.56
  513.1 1.1 fusion.56
  515.4 1.1 fusion.56
  517.7 1.1 fusion.56
  520.0 1.1 fusion.56
  522.4 1.1 fusion.56
  524.7 1.1 fusion.56
  527.0 1.1 fusion.56
  529.3 1.1 fusion.56
  531.7 1.1 fusion.56
  534.0 1.1 fusion.56
  536.3 1.1 fusion.56
  538.6 1.1 fusion.56
  541.0 1.1 fusion.56
  543.3 1.1 fusion.56
  545.6 1.1 fusion.56
  547.9 1.1 fusion.56
  550.2 1.1 fusion.56
  552.6 1.1 fusion.56
  554.9 1.1 fusion.56
  557.2 1.1 fusion.56
  559.5 1.1 fusion.56
  561.9 1.1 fusion.56
  564.2 1.1 fusion.56
  566.5 1.1 fusion.56
  568.8 1.1 fusion.56
  571.2 1.1 fusion.56
  573.5 1.1 fusion.56
  575.8 1.1 fusion.56
  578.1 1.1 fusion.56
  580.4 1.1 fusion.56
  582.8 1.1 fusion.56
  585.1 1.1 fusion.56
  587.4 1.1 fusion.56
  589.7 1.1 fusion.56
  592.1 1.1 fusion.56
  635.0 148.5 %while.66 = (s32[]{:T(128)}, f32[128,128]{1,0:T(8,128)S(1)}, f32[128,128]{1,0:T(8,128)S(1)}, s32[64]{0:T(128)S(1)}, s32[]{:T(128)}, /*index=5*/f32[64,128,128]{2...) while((s32[]{:T(128)}, f32[128,128]{1,0:T(8,128)S(1)}, ...), condition=%wide.region_5.6_spmd.clone, body=%wide.region_4.5_spmd.clone.sunk | while | flops 245764 | bytes 655521 | solution.py:119
  (299 shorter events, 204.7 us)
Async XLA Ops:
  7.2 6.2 copy-start
  7.2 6.2 copy-start.4
  7.2 6.2 copy-start.5
  7.2 182.0 %all-gather.11.cloned.1.call-start = ((), (), s32[]{:S(2)}) async-start(), calls=%async_computation.1 | async-start | bytes 4259840 | tf_op jit(solution)/shard_map/all_gather | solution.py:100
  7.2 6.2 copy-start.6
  8.1 5.2 collective-permute-start
  19.8 5.7 copy-start.1
  19.8 5.7 copy-start.2
  19.8 5.4 collective-permute-start.1
  47.5 0.8 copy-start.3
  64.5 185.2 %all-gather.13.cloned.1.call-start = ((), (), s32[]{:S(2)}) async-start(), calls=%async_computation.2 | async-start | bytes 4259840 | tf_op jit(solution)/shard_map/all_gather | solution.py:101
  65.2 263.4 %all-gather.15.cloned.1.call-start = ((), (), s32[]{:S(2)}) async-start(), calls=%async_computation.3 | async-start | bytes 4259840 | tf_op jit(solution)/shard_map/all_gather | solution.py:95
  65.9 341.5 %all-gather.17.cloned.1.call-start = ((), (), s32[]{:S(2)}) async-start(), calls=%async_computation.4 | async-start | bytes 4259840 | tf_op jit(solution)/shard_map/all_gather | solution.py:96
  69.0 120.2 %all-to-all-start = ((f32[64,1,128,128]{3,2,1,0:T(8,128)}), f32[64,1,128,128]{3,2,1,0:T(8,128)}, u32[]{:S(2)}, u32[]{:S(2)}) async-start(f32[64,1,128,128]{3,2,1,0:T(8,128)} %stack.16), calls=%async_computation | async-start | bytes 8388608 | tf_op jit(solution)/shard_map/all_to_all | solution.py:98
  82.7 403.6 %all-gather.19.cloned.1.call-start = ((), (), s32[]{:S(2)}) async-start(), calls=%async_computation.5 | async-start | bytes 4259840 | tf_op jit(solution)/shard_map/all_gather | solution.py:102
Sparse Core Ops, SparseCore 0:
  64.6 102.8 all-gather.10
  170.8 78.8 all-gather.12
  252.4 76.1 all-gather.14
  331.3 76.1 all-gather.16
  410.1 76.1 all-gather.18
